TPU v7x, 256 devices: a whole 4x4x8 slice. The times are simulated.
256 devices in a mesh: ctx: 32 (over z, y), head: 8 (over x, core).
Axes of the slice: x: 4, y: 4, z: 8, core: 2. Of those that a mesh axis runs over, the one named last changes fastest.
Arguments:
- queries: bfloat16 [65536, 8, 128], P('ctx', 'head'), may hold values from -4 to 4
- keys: bfloat16 [65536, 128], P('ctx'), may hold values from -5 to 5
- values: bfloat16 [65536, 128], P('ctx'), may hold values from -6 to 6
- dout: bfloat16 [65536, 8, 128], P('ctx', 'head'), may hold values from -6 to 6
- selected: int32 [128, 3], P('ctx'), may hold values from 0 to 126, as said below
Outputs:
- grad_queries: bfloat16 [65536, 8, 128], P('ctx', 'head')
- grad_keys: bfloat16 [65536, 128], P('ctx')
- grad_values: bfloat16 [65536, 128], P('ctx')
Inputs may be any that keep to these rules, and one draw needn't show every extreme that they name: `selected`: each entry of row g is either g itself, meaning no block, or an earlier block (below g); the entries of a row that are not g differ; g itself appears only in rows that have fewer than 3 earlier blocks to choose from. Over the 4 rows of one index of ctx, all entries that lie on one other index of ctx (block // 4) name the same block, so one index of ctx reads at most one block from each other index. Every row from 4 on names exactly one block among the first 4. The last row names block 126.
All inputs are finite; a program needn't handle non-finite values.
Results may differ from a plain program's by a relative error of at most 0.015.
Values may be sent and summed in bfloat16 or wider, within the bound.
A program may use at most 192 MiB of HBM per device.

v0:
```python
import math

import jax
import jax.numpy as jnp
from jax import lax
from jax.sharding import PartitionSpec as P


def block_grads(q_rows, do_rows, key_rows, value_rows, allowed, scaling):
    scores = jnp.einsum("id,jd->ij", q_rows, key_rows, preferred_element_type=jnp.float32) * scaling
    masked = jnp.where(allowed, scores, -jnp.inf)
    row_max = jnp.max(masked, axis=1, keepdims=True)
    exp_terms = jnp.where(allowed, jnp.exp(masked - row_max), jnp.float32(0.0))
    weights = exp_terms / jnp.sum(exp_terms, axis=1, keepdims=True)
    probs_b = weights.astype(jnp.bfloat16)
    attended = jnp.dot(probs_b, value_rows, preferred_element_type=jnp.float32)
    row_delta = jnp.sum(do_rows.astype(jnp.float32) * attended, axis=1, keepdims=True)
    dprobs = jnp.einsum("id,jd->ij", do_rows, value_rows, preferred_element_type=jnp.float32)
    dscores = (weights * (dprobs - row_delta)).astype(jnp.bfloat16)
    grad_q = (jnp.dot(dscores, key_rows, preferred_element_type=jnp.float32) * scaling).astype(
        jnp.bfloat16
    )
    grad_k = jnp.einsum("ij,id->jd", dscores, q_rows, preferred_element_type=jnp.float32) * scaling
    grad_v = jnp.einsum("ij,id->jd", probs_b, do_rows, preferred_element_type=jnp.float32)
    return (grad_q, grad_k, grad_v)


def add_returns(asked_for, returned, blocks_here):
    target = jnp.where(asked_for >= 0, asked_for, blocks_here)
    shape_out = (blocks_here + 1,) + returned.shape[1:]
    return jnp.zeros(shape_out, jnp.float32).at[target].add(returned)[:blocks_here]


def body(queries, keys, values, dout, selected):
    tok_rows, head_count, feature = queries.shape
    blocks_here = selected.shape[0]
    block_len = tok_rows // blocks_here
    ctx_count = lax.axis_size("ctx")
    ctx_self = lax.axis_index("ctx")
    scaling = 1.0 / math.sqrt(feature)
    local_ids = jnp.arange(blocks_here, dtype=jnp.int32)
    block_ids = ctx_self * blocks_here + local_ids
    owners = selected // blocks_here
    inside = selected % blocks_here
    vacant = selected == block_ids[:, None]
    distant = (owners != ctx_self) & jnp.logical_not(vacant)
    peer_ids = jnp.arange(ctx_count, dtype=jnp.int32)
    matches = distant[:, :, None] & (owners[:, :, None] == peer_ids[None, None, :])
    wanted = jnp.max(jnp.where(matches, inside[:, :, None], -1), axis=(0, 1))
    asked_for = lax.all_to_all(
        wanted.reshape(ctx_count, 1), "ctx", split_axis=0, concat_axis=0, tiled=True
    ).reshape(ctx_count)
    present = asked_for >= 0
    slot_ids = jnp.maximum(asked_for, 0)
    key_blocks = keys.reshape(blocks_here, block_len, feature)
    value_blocks = values.reshape(blocks_here, block_len, feature)
    send_keys = jnp.where(present[:, None, None], key_blocks[slot_ids], 0)
    send_values = jnp.where(present[:, None, None], value_blocks[slot_ids], 0)
    far_keys, far_values = (
        lax.all_to_all(send_keys, "ctx", split_axis=0, concat_axis=0, tiled=True),
        lax.all_to_all(send_values, "ctx", split_axis=0, concat_axis=0, tiled=True),
    )
    table_keys = jnp.concatenate([key_blocks, far_keys], axis=0)
    table_values = jnp.concatenate([value_blocks, far_values], axis=0)
    table_index = jnp.where(
        vacant, local_ids[:, None], jnp.where(owners == ctx_self, inside, blocks_here + owners)
    )
    listed_all = jnp.concatenate([table_index, local_ids[:, None]], axis=1)
    alive_all = jnp.concatenate(
        [jnp.logical_not(vacant), jnp.ones((blocks_here, 1), jnp.bool_)], axis=1
    )
    row_pos = jnp.arange(block_len * head_count) // head_count
    col_pos = jnp.arange(4 * block_len)
    col_block = col_pos // block_len
    col_row = col_pos % block_len

    def per_block(running, number):
        acc_keys, acc_values = running
        listed = listed_all[number]
        alive_flags = alive_all[number]
        allowed = jnp.where(
            col_block[None, :] == 3,
            col_row[None, :] <= row_pos[:, None],
            alive_flags[col_block][None, :],
        )
        q_rows = lax.dynamic_slice_in_dim(queries, number * block_len, block_len, 0).reshape(
            block_len * head_count, feature
        )
        do_rows = lax.dynamic_slice_in_dim(dout, number * block_len, block_len, 0).reshape(
            block_len * head_count, feature
        )
        key_rows = table_keys[listed].reshape(4 * block_len, feature)
        value_rows = table_values[listed].reshape(4 * block_len, feature)
        grad_q, grad_k, grad_v = block_grads(
            q_rows, do_rows, key_rows, value_rows, allowed, scaling
        )
        acc_keys = acc_keys.at[listed].add(grad_k.reshape(4, block_len, feature))
        acc_values = acc_values.at[listed].add(grad_v.reshape(4, block_len, feature))
        return ((acc_keys, acc_values), grad_q)

    start = jnp.zeros((blocks_here + ctx_count, block_len, feature), jnp.float32)
    (acc_keys, acc_values), grads_q = lax.scan(per_block, (start, start), local_ids)
    grad_queries = grads_q.reshape(tok_rows, head_count, feature)
    back_keys, back_values = (
        lax.all_to_all(
            acc_keys[blocks_here:].astype(jnp.bfloat16),
            "ctx",
            split_axis=0,
            concat_axis=0,
            tiled=True,
        ).astype(jnp.float32),
        lax.all_to_all(
            acc_values[blocks_here:].astype(jnp.bfloat16),
            "ctx",
            split_axis=0,
            concat_axis=0,
            tiled=True,
        ).astype(jnp.float32),
    )
    own_keys = add_returns(asked_for, back_keys, blocks_here) + acc_keys[:blocks_here]
    own_values = add_returns(asked_for, back_values, blocks_here) + acc_values[:blocks_here]
    total_keys, total_values = (
        lax.psum(own_keys.reshape(tok_rows, feature).astype(jnp.bfloat16), "head").astype(
            jnp.float32
        ),
        lax.psum(own_values.reshape(tok_rows, feature).astype(jnp.bfloat16), "head").astype(
            jnp.float32
        ),
    )
    grad_keys = total_keys.astype(jnp.bfloat16)
    grad_values = total_values.astype(jnp.bfloat16)
    return (grad_queries, grad_keys, grad_values)


def solution(mesh):
    return jax.shard_map(
        body,
        mesh=mesh,
        in_specs=(
            P("ctx", "head", None),
            P("ctx", None),
            P("ctx", None),
            P("ctx", "head", None),
            P("ctx", None),
        ),
        out_specs=(P("ctx", "head", None), P("ctx", None), P("ctx", None)),
        check_vma=False,
    )
```

profile of v0, /device:TPU:1, one launch (start us, length us, event | category | flops | bytes accessed | tf_op | source)
XLA Modules:
  0.0 739.6 jit_solution(18308067598460061203)
XLA Ops:
  9.1 20.4 %all_to_all.32 = s32[32,1,1]{2,1,0:T(1,128)S(1)} all-to-all(s32[32,1,1]{2,1,0:T(1,128)S(1)} %copy.27), channel_id=1, replica_groups=mesh['ctx'=32,'head'=8] {'ctx'}, dimensions={0} | all-to-all | bytes 256 | tf_op jit(solution)/shard_map/all_to_all | solution.py:50
  30.2 4.1 gather_fusion.2
  34.3 3.1 gather_fusion.3
  38.1 5.1 broadcast_select_fusion
  43.2 96.4 %all_to_all.33 = bf16[32,512,128]{2,1,0:T(8,128)(2,1)} all-to-all(bf16[32,512,128]{2,1,0:T(8,128)(2,1)S(1)} %get-tuple-element.250), channel_id=1, replica_groups=mesh['ctx'=32,'head'=8] {'ctx'}, dimensions={0} | all-to-all | bytes 8388608 | tf_op jit(solution)/shard_map/all_to_all | solution.py:60
  139.6 7.0 all-to-all-start.2
  146.8 4.8 pad_maximum_fusion
  151.5 87.9 %all-to-all-done.2 = bf16[32,512,128]{2,1,0:T(8,128)(2,1)} async-done(((bf16[32,512,128]{2,1,0:T(8,128)(2,1)}), bf16[32,512,128]{2,1,0:T(8,128)(2,1)}, u32[]{:S(2)}, u32[]{:S(2)}) %all-to-all-start.2) | async-done | bytes 4194336 | tf_op jit(solution)/shard_map/all_to_all | solution.py:61
  239.4 4.8 pad_maximum_fusion.1
  244.2 4.7 broadcast_in_dim.108
  249.0 4.8 broadcast_in_dim.108.clone
  253.7 183.8 %while.16 = (s32[]{:T(128)}, f32[36,512,128]{2,1,0:T(8,128)}, f32[36,512,128]{2,1,0:T(8,128)}, bf16[4,512,128]{2,1,0:T(8,128)(2,1)}, s32[4]{0:T(128)S(1)}, /*ind...) while((s32[]{:T(128)}, f32[36,512,128]{2,1,0:T(8,128)}, ...), condition=%wide.region_7.8_spmd.clone.clone, body=%wide.region_1.7_spmd.clone.clone.sunk | while | flops 1644297728 | bytes 93686752 | solution.py:102
  256.9 2.6 select_reduce_fusion.3
  260.2 3.0 gather_fusion
  263.2 2.4 fusion.94
  267.7 2.6 fusion.97
  270.3 2.5 copy.36
  276.0 3.0 scatter_fusion.1
  279.1 6.2 broadcast_divide_fusion.2
  285.4 3.0 gather_fusion.1
  288.4 3.2 fusion.96
  294.2 3.0 scatter_fusion
  297.2 2.4 fusion.99
  302.8 2.6 select_reduce_fusion.3
  306.1 3.0 gather_fusion
  309.2 2.4 fusion.94
  313.7 2.6 fusion.97
  316.2 2.5 copy.36
  322.0 3.0 scatter_fusion.1
  324.9 6.2 broadcast_divide_fusion.2
  331.2 3.0 gather_fusion.1
  334.2 3.2 fusion.96
  340.0 3.0 scatter_fusion
  348.7 2.6 select_reduce_fusion.3
  351.9 3.0 gather_fusion
  355.0 2.4 fusion.94
  359.5 2.6 fusion.97
  362.0 2.5 copy.36
  367.8 3.1 scatter_fusion.1
  370.8 6.2 broadcast_divide_fusion.2
  377.1 3.0 gather_fusion.1
  380.1 3.2 fusion.96
  385.9 3.0 scatter_fusion
  394.6 2.6 select_reduce_fusion.3
  397.9 3.0 gather_fusion
  400.9 2.4 fusion.94
  405.4 2.6 fusion.97
  408.0 2.5 copy.36
  413.7 3.2 scatter_fusion.1
  416.9 6.2 broadcast_divide_fusion.2
  423.2 3.0 gather_fusion.1
  426.2 3.2 fusion.96
  432.0 3.2 scatter_fusion
  437.6 6.1 slice.62
  443.6 7.1 all-to-all-start.4
  450.7 6.0 slice.63
  456.7 85.5 %all-to-all-done.4 = bf16[32,512,128]{2,1,0:T(8,128)(2,1)} async-done(((bf16[32,512,128]{2,1,0:T(8,128)(2,1)}), bf16[32,512,128]{2,1,0:T(8,128)(2,1)}, u32[]{:S(2)}, u32[]{:S(2)}) %all-to-all-start.4) | async-done | bytes 4194336 | tf_op jit(solution)/shard_map/all_to_all | solution.py:112
  542.3 7.6 %all-to-all-start.3 = ((bf16[32,512,128]{2,1,0:T(8,128)(2,1)}), bf16[32,512,128]{2,1,0:T(8,128)(2,1)}, u32[]{:S(2)}, u32[]{:S(2)}) async-start(bf16[32,512,128]{2,1,0:T(8,128)(2,1)} %slice.63), calls=%async_computation.3 | async-start | bytes 8388608 | tf_op jit(solution)/shard_map/all_to_all | solution.py:105
  549.9 6.5 convert_element_type.45
  556.6 11.7 %scatter_fusion.3 = f32[5,512,128]{2,1,0:T(8,128)S(1)} fusion(f32[5,512,128]{2,1,0:T(8,128)S(1)} %broadcast.179.clone.1, s32[32]{0:T(128)S(1)} %get-tuple-element.247, f32[32,512,128]{2,1,0:T(8,128)} %convert_element_type.45), kind=kCustom, calls=%fused_computation.7 | custom fusion | flops 2097152 | bytes 25165952 | tf_op jit(solution)/shard_map/scatter-add | solution.py:31
  570.4 72.1 %all-to-all-done.3 = bf16[32,512,128]{2,1,0:T(8,128)(2,1)} async-done(((bf16[32,512,128]{2,1,0:T(8,128)(2,1)}), bf16[32,512,128]{2,1,0:T(8,128)(2,1)}, u32[]{:S(2)}, u32[]{:S(2)}) %all-to-all-start.3) | async-done | bytes 4194336 | tf_op jit(solution)/shard_map/all_to_all | solution.py:105
  642.5 6.5 convert_element_type.42
  649.1 11.7 %scatter_fusion.2 = f32[5,512,128]{2,1,0:T(8,128)S(1)} fusion(f32[5,512,128]{2,1,0:T(8,128)S(1)} %broadcast.179.clone, s32[32]{0:T(128)S(1)} %get-tuple-element.247, f32[32,512,128]{2,1,0:T(8,128)} %convert_element_type.42), kind=kCustom, calls=%fused_computation.6 | custom fusion | flops 2097152 | bytes 25165952 | tf_op jit(solution)/shard_map/scatter-add | solution.py:31
  663.0 66.1 %all-reduce.4.cloned.1.call-done = (bf16[2048,128]{1,0:T(8,128)(2,1)}, bf16[2048,128]{1,0:T(8,128)(2,1)}) async-done(((bf16[2048,128]{1,0:T(8,128)(2,1)}, bf16[2048,128]{1,0:T(8,128)(2,1)}), (bf16[2048,128]{1,0:T(8,128)(2,1)}, bf16[2048,128]{1,0:T(8,128)(2,1)})) %all-reduce.4.cloned.1.call-update) | async-done | bytes 1048592 | tf_op jit(solution)/shard_map/psum | solution.py:123
  (113 shorter events, 56.0 us)
Async XLA Ops:
  30.2 4.1 copy-start.3
  139.6 7.1 copy-start.2
  139.6 99.7 %all-to-all-start.2 = ((bf16[32,512,128]{2,1,0:T(8,128)(2,1)}), bf16[32,512,128]{2,1,0:T(8,128)(2,1)}, u32[]{:S(2)}, u32[]{:S(2)}) async-start(bf16[32,512,128]{2,1,0:T(8,128)(2,1)} %get-tuple-element.249), calls=%async_computation.2 | async-start | bytes 8388608 | tf_op jit(solution)/shard_map/all_to_all | solution.py:61
  263.2 2.5 copy-start.4
  265.7 2.0 copy-start.1
  288.4 3.5 copy-start
  309.1 2.5 copy-start.4
  311.6 2.0 copy-start.1
  334.2 3.5 copy-start
  354.9 2.5 copy-start.4
  357.4 2.0 copy-start.1
  380.1 3.5 copy-start
  400.9 2.5 copy-start.4
  403.4 2.0 copy-start.1
  426.1 3.5 copy-start
  443.6 98.7 %all-to-all-start.4 = ((bf16[32,512,128]{2,1,0:T(8,128)(2,1)}), bf16[32,512,128]{2,1,0:T(8,128)(2,1)}, u32[]{:S(2)}, u32[]{:S(2)}) async-start(bf16[32,512,128]{2,1,0:T(8,128)(2,1)} %slice.62), calls=%async_computation.4 | async-start | bytes 8388608 | tf_op jit(solution)/shard_map/all_to_all | solution.py:112
  542.3 100.3 %all-to-all-start.3 = ((bf16[32,512,128]{2,1,0:T(8,128)(2,1)}), bf16[32,512,128]{2,1,0:T(8,128)(2,1)}, u32[]{:S(2)}, u32[]{:S(2)}) async-start(bf16[32,512,128]{2,1,0:T(8,128)(2,1)} %slice.63), calls=%async_computation.3 | async-start | bytes 8388608 | tf_op jit(solution)/shard_map/all_to_all | solution.py:105
  549.9 179.2 %all-reduce.4.cloned.1.call-start = ((), (), s32[]{:S(2)}) async-start(), calls=%async_computation.5 | async-start | bytes 2097152 | tf_op jit(solution)/shard_map/psum | solution.py:123
Sparse Core Ops, SparseCore 0:
  663.1 65.9 all-reduce.3
where the time goes:
time: 743 us; the launch traced here: 740 us
  waiting for transfers between devices  312 us (42%)
  other arithmetic  135 us (18%)
  blocking collectives  117 us (16%)
  local copies, waits for them, and re-layouts  78.2 us (11%)
  matrix products  50.8 us (7%)
  starting transfers between devices  21.8 us (3%)
  between operations  14.1 us (2%)
  loops' own time  10.9 us (1%)
    all_to_all x1, blocking collectives, body(): lax.all_to_all(send_keys, 'ctx', split_axis=0, concat_axis=0, tiled=True)  96.4 us
    all_to_all x1, waiting for transfers between devices, body(): lax.all_to_all(send_values, 'ctx', split_axis=0, concat_axis=0, tiled=True)  87.9 us
    all_to_all x1, waiting for transfers between devices, body(): lax.all_to_all(acc_values[blocks_here:].astype(jnp.bfloat16), 'ctx', spli...  85.5 us
    all_to_all x1, waiting for transfers between devices, body(): lax.all_to_all(acc_keys[blocks_here:].astype(jnp.bfloat16), 'ctx', split_...  72.1 us
    psum x1, waiting for transfers between devices, body(): lax.psum(own_keys.reshape(tok_rows, feature).astype(jnp.bfloat16), 'head')  66.1 us
    div x4, other arithmetic, block_grads(): weights = exp_terms / jnp.sum(exp_terms, axis=1, keepdims=True)  24.6 us
    scatter-add x2, other arithmetic, add_returns(): jnp.zeros(shape_out, jnp.float32).at[target].add(returned)[:blocks_here]  23.4 us
    all_to_all x1, blocking collectives, body(): lax.all_to_all(wanted.reshape(ctx_count, 1), 'ctx', split_axis=0, concat_...  20.4 us
  transfers between devices with their start and end apart: 4, of which 4 were waited for; matrix products, arithmetic and copies ran while one was open for 4% of the time, Pallas kernels for 0%

commit v1 on v0

v1 whole, which is shorter than its diff:
```python
import functools
import math

import jax
import jax.numpy as jnp
from jax import lax
from jax.experimental import pallas as pl
from jax.experimental.pallas import tpu as pltpu
from jax.sharding import PartitionSpec as P

MESH = pl.DeviceIdType.MESH
F32 = jnp.float32
BF16 = jnp.bfloat16
VM = pl.BlockSpec(memory_space=pltpu.VMEM)
SM = pl.BlockSpec(memory_space=pltpu.SMEM)


def greet(n):
    me = lax.axis_index("ctx")
    head = lax.axis_index("head")
    chip, core = head // 2, head % 2
    barrier = pltpu.get_barrier_semaphore()

    def hello(step, carry):
        pl.semaphore_signal(
            barrier, inc=1, device_id={"ctx": lax.rem(me + step, n)}, device_id_type=MESH
        )
        return carry

    lax.fori_loop(1, n, hello, 0)
    for step in range(1, 4):
        pl.semaphore_signal(
            barrier,
            inc=1,
            device_id={"head": lax.rem(chip + step, 4) * 2 + core},
            device_id_type=MESH,
        )
    pl.semaphore_signal(
        barrier, inc=1, device_id={"head": chip * 2 + 1 - core}, device_id_type=MESH
    )
    pl.semaphore_wait(barrier, n - 1 + 4)
    return me, chip, core


def fetch_kernel(
    n,
    cidx,
    ask,
    keys,
    values,
    queries,
    dout,
    q_out,
    do_out,
    kv_out,
    asked,
    table,
    send,
    comp,
    ask_send,
    ask_recv,
    kv_send,
    kv_recv,
    x_send,
    x_recv,
    core_send,
    core_recv,
):
    rows = keys.shape[2]
    me, chip, core = greet(n)

    def to_chip(step, slot, src, dst):
        peer = lax.rem(chip + step, 4)
        return pltpu.make_async_remote_copy(
            src_ref=src(peer),
            dst_ref=dst,
            send_sem=x_send.at[slot, step],
            recv_sem=x_recv.at[slot, step],
            device_id={"head": peer * 2 + core},
            device_id_type=MESH,
        )

    def ask_copy(owner, place):
        return pltpu.make_async_remote_copy(
            src_ref=ask.at[owner],
            dst_ref=asked.at[place],
            send_sem=ask_send.at[owner],
            recv_sem=ask_recv.at[place],
            device_id={"ctx": owner},
            device_id_type=MESH,
        )

    def kv_copy(reader, place):
        return pltpu.make_async_remote_copy(
            src_ref=send.at[reader],
            dst_ref=table.at[place],
            send_sem=kv_send.at[reader],
            recv_sem=kv_recv.at[place],
            device_id={"ctx": reader},
            device_id_type=MESH,
        )

    def start_ask(owner, carry):
        ask_copy(owner, me).start()
        return carry

    lax.fori_loop(0, me, start_ask, 0)
    q_copies = []
    for step in (1, 3, 2):
        q_copies.append(to_chip(step, 0, lambda peer: queries.at[peer], q_out.at[chip]))
        q_copies.append(to_chip(step, 1, lambda peer: dout.at[peer], do_out.at[chip]))
    for copy in q_copies:
        copy.start()
    q_out[chip] = queries[chip]
    do_out[chip] = dout[chip]
    part = core * 4 + chip
    for b in range(4):
        table[n + b, 0] = keys[b, part]
        table[n + b, 1] = values[b, part]

    def serve(reader, carry):
        ask_copy(reader, reader).wait_recv()
        wish = asked[reader].astype(F32)
        masks = [jnp.where(wish == b, 1.0, 0.0).astype(BF16) for b in range(4)]
        for half in range(2):
            for g in range(rows // 16):
                span = pl.ds(16 * g, 16)
                total = table[n, half, span] * masks[0]
                for b in range(1, 4):
                    total = total + table[n + b, half, span] * masks[b]
                send[reader, half, span] = total
        kv_copy(reader, me).start()
        return carry

    lax.fori_loop(me + 1, n, serve, 0)

    def got_kv(owner, carry):
        kv_copy(owner, owner).wait_recv()
        return carry

    lax.fori_loop(0, me, got_kv, 0)

    for x in range(4):
        for t in range(3):
            comp[x, t] = table[cidx[x * 3 + t]]
    kv_copies = [
        to_chip(step, 2, lambda peer: comp.at[peer], kv_out.at[:, :, core, chip])
        for step in (1, 3, 2)
    ]
    for copy in kv_copies:
        copy.start()
    for t in range(3):
        for half in range(2):
            kv_out[t, half, core, chip] = comp[chip, t, half]
    for copy in kv_copies:
        copy.wait_recv()
    swap = pltpu.make_async_remote_copy(
        src_ref=kv_out.at[:, :, core],
        dst_ref=kv_out.at[:, :, core],
        send_sem=core_send,
        recv_sem=core_recv,
        device_id={"head": chip * 2 + 1 - core},
        device_id_type=MESH,
    )
    swap.start()
    for copy in q_copies:
        copy.wait()
    for copy in kv_copies:
        copy.wait_send()

    def sent_ask(owner, carry):
        ask_copy(owner, me).wait_send()
        return carry

    lax.fori_loop(0, me, sent_ask, 0)

    def sent_kv(reader, carry):
        kv_copy(reader, me).wait_send()
        return carry

    lax.fori_loop(me + 1, n, sent_kv, 0)
    swap.wait()


def attend_kernel(
    scaling, meta, q_ref, do_ref, kv_ref, k_own, v_own, gq_ref, terms, scores, dprobs, acc, k_turned
):
    head = pl.program_id(0)
    length = q_ref.shape[1]
    factor = scaling * math.log2(math.e)
    nt = (((1,), (1,)), ((), ()))

    def key_rows(t):
        return kv_ref[t, 0] if t < 3 else k_own[0]

    def value_rows(t):
        return kv_ref[t, 1] if t < 3 else v_own[0]

    @pl.when(head == 0)
    def _():
        acc[...] = jnp.zeros_like(acc)
        for t in range(4):
            k_turned[t] = key_rows(t).T

    q = q_ref[0]
    do = do_ref[0]
    live = [meta[t] > 0 for t in range(3)]
    top = None
    for t in range(4):
        s = lax.dot_general(key_rows(t), q, nt, preferred_element_type=F32)
        if t == 3:
            col = lax.broadcasted_iota(jnp.int32, (length, length), 0)
            row = lax.broadcasted_iota(jnp.int32, (length, length), 1)
            s = jnp.where(col <= row, s, -jnp.inf)
        scores[t] = s
        best = jnp.max(s, axis=0, keepdims=True)
        if t < 3:
            best = jnp.where(live[t], best, -jnp.inf)
        top = best if top is None else jnp.maximum(top, best)
    top = top * factor
    total = jnp.zeros((1, length), F32)
    weighted = jnp.zeros((1, length), F32)
    for t in range(4):
        shift = jnp.where(live[t], top, jnp.inf) if t < 3 else top
        e = jnp.exp2(scores[t] * factor - shift)
        dp = lax.dot_general(value_rows(t), do, nt, preferred_element_type=F32)
        total = total + jnp.sum(e, axis=0, keepdims=True)
        weighted = weighted + jnp.sum(e * dp, axis=0, keepdims=True)
        scores[t] = e
        dprobs[t] = dp
    inverse = 1.0 / total
    delta = weighted * inverse
    gq = jnp.zeros((q.shape[1], length), F32)
    for t in range(4):
        p = scores[t] * inverse
        ds = (p * (dprobs[t] - delta)).astype(BF16)
        acc[t, 1] += jnp.dot(p.astype(BF16), do, preferred_element_type=F32)
        acc[t, 0] += jnp.dot(ds, q, preferred_element_type=F32)
        gq = gq + jnp.dot(k_turned[t], ds, preferred_element_type=F32)
    gq_ref[0] = (gq * scaling).T.astype(BF16)

    @pl.when(head == pl.num_programs(0) - 1)
    def _():
        for t in range(4):
            terms[t, 0] = (acc[t, 0] * scaling).astype(BF16)
            terms[t, 1] = acc[t, 1].astype(BF16)


def return_kernel(
    n,
    tix,
    terms,
    gq,
    asked,
    gq_out,
    gk_out,
    gv_out,
    pair,
    outgoing,
    incoming,
    send,
    back,
    own,
    final,
    back_send,
    back_recv,
    x_send,
    x_recv,
    core_send,
    core_recv,
):
    rows = terms.shape[4]
    me, chip, core = greet(n)

    def to_chip(step, slot, src, dst):
        peer = lax.rem(chip + step, 4)
        return pltpu.make_async_remote_copy(
            src_ref=src(peer),
            dst_ref=dst,
            send_sem=x_send.at[slot, step],
            recv_sem=x_recv.at[slot, step],
            device_id={"head": peer * 2 + core},
            device_id_type=MESH,
        )

    def to_core(slot, src, dst):
        return pltpu.make_async_remote_copy(
            src_ref=src,
            dst_ref=dst,
            send_sem=core_send.at[slot],
            recv_sem=core_recv.at[slot],
            device_id={"head": chip * 2 + 1 - core},
            device_id_type=MESH,
        )

    def back_copy(owner, place):
        return pltpu.make_async_remote_copy(
            src_ref=send.at[owner],
            dst_ref=back.at[place],
            send_sem=back_send.at[owner],
            recv_sem=back_recv.at[place],
            device_id={"ctx": owner},
            device_id_type=MESH,
        )

    merge = to_core(0, terms.at[:, :, 1 - core], pair)
    merge.start()
    for x in range(4):
        incoming[x, 4] = jnp.zeros_like(incoming[x, 4])
    merge.wait()
    for t in range(4):
        for half in range(2):
            for x in range(4):
                total = terms[t, half, core, x].astype(F32) + pair[t, half, x].astype(F32)
                outgoing[x, t, half] = total.astype(BF16)
    spread = [
        to_chip(step, 0, lambda peer: outgoing.at[peer], incoming.at[chip, pl.ds(0, 4)])
        for step in (1, 3, 2)
    ]
    for copy in spread:
        copy.start()
    for t in range(4):
        incoming[chip, t] = outgoing[chip, t]
    gq_copies = [
        to_chip(step, 1, lambda peer: gq.at[peer], gq_out.at[chip]) for step in (1, 3, 2)
    ]
    for copy in spread:
        copy.wait_recv()

    def collect(place):
        total = incoming[0, tix[place]].astype(F32)
        for x in range(1, 4):
            total = total + incoming[x, tix[x * (n + 4) + place]].astype(F32)
        return total

    def give_back(owner, carry):
        send[owner] = collect(owner).astype(BF16)
        back_copy(owner, me).start()
        return carry

    lax.fori_loop(0, me, give_back, 0)
    for copy in gq_copies:
        copy.start()
    gq_out[chip] = gq[chip]
    for b in range(4):
        own[b] = collect(n + b)

    def take_back(reader, carry):
        back_copy(reader, reader).wait_recv()
        wish = asked[reader].astype(F32)
        masks = [jnp.where(wish == b, 1.0, 0.0) for b in range(4)]
        for half in range(2):
            for g in range(rows // 16):
                span = pl.ds(16 * g, 16)
                part = back[reader, half, span].astype(F32)
                for b in range(4):
                    own[b, half, span] += part * masks[b]
        return carry

    lax.fori_loop(me + 1, n, take_back, 0)
    for b in range(4):
        final[0, b] = own[b, 0].astype(BF16)
        final[1, b] = own[b, 1].astype(BF16)
    shares = []
    for step in (1, 3, 2):
        shares.append(to_chip(step, 2, lambda peer: final.at[0], gk_out.at[:, core, chip]))
        shares.append(to_chip(step, 3, lambda peer: final.at[1], gv_out.at[:, core, chip]))
    for copy in shares:
        copy.start()
    for b in range(4):
        gk_out[b, core, chip] = final[0, b]
        gv_out[b, core, chip] = final[1, b]
    for copy in shares:
        copy.wait_recv()
    swap_k = to_core(1, gk_out.at[:, core], gk_out.at[:, core])
    swap_v = to_core(2, gv_out.at[:, core], gv_out.at[:, core])
    swap_k.start()
    swap_v.start()
    for copy in shares + spread:
        copy.wait_send()
    for copy in gq_copies:
        copy.wait()

    def sent_back(owner, carry):
        back_copy(owner, me).wait_send()
        return carry

    lax.fori_loop(0, me, sent_back, 0)
    swap_k.wait()
    swap_v.wait()


def body(queries, keys, values, dout, selected):
    tok, _, feature = queries.shape
    blocks = selected.shape[0]
    length = tok // blocks
    rows = length // 8
    n = lax.axis_size("ctx")
    me = lax.axis_index("ctx")
    chip = lax.axis_index("head") // 2
    scaling = 1.0 / math.sqrt(feature)
    dma = pltpu.SemaphoreType.DMA

    local = jnp.arange(blocks, dtype=jnp.int32)
    vacant = selected == (me * blocks + local)[:, None]
    owners = selected // blocks
    inside = selected % blocks
    distant = (owners != me) & jnp.logical_not(vacant)
    near = (owners == me) & jnp.logical_not(vacant)
    peers = jnp.arange(n, dtype=jnp.int32)
    hits = distant[:, :, None] & (owners[:, :, None] == peers)
    wanted = jnp.max(jnp.where(hits, inside[:, :, None], -1), axis=(0, 1))
    ask = jnp.broadcast_to(wanted.astype(BF16)[:, None, None], (n, 16, 128))
    cidx = jnp.where(vacant, n + local[:, None], jnp.where(owners == me, n + inside, owners))
    near_hits = near[:, :, None] & (inside[:, :, None] == local)
    tcol = jnp.arange(3, dtype=jnp.int32)[None, :, None]
    far_t = jnp.min(jnp.where(hits, tcol, 4), axis=1)
    near_t = jnp.min(jnp.where(near_hits, tcol, 4), axis=1)
    near_t = jnp.where(local[:, None] == local[None, :], 3, near_t)
    tix = jnp.concatenate([far_t, near_t], axis=1).reshape(-1)
    alive = lax.dynamic_index_in_dim(
        jnp.logical_not(vacant).astype(jnp.int32), chip, 0, keepdims=False
    )
    meta = jnp.concatenate([alive, chip.astype(jnp.int32)[None]])

    q_blocks = queries.reshape(blocks, length, feature)
    do_blocks = dout.reshape(blocks, length, feature)
    k_blocks = keys.reshape(blocks, length, feature)
    v_blocks = values.reshape(blocks, length, feature)
    heads_shape = jax.ShapeDtypeStruct((4, length, feature), BF16)
    q_mine, do_mine, kv_list, asked = pl.pallas_call(
        functools.partial(fetch_kernel, n),
        out_shape=(
            heads_shape,
            heads_shape,
            jax.ShapeDtypeStruct((3, 2, 2, 4, rows, feature), BF16),
            jax.ShapeDtypeStruct((n, 16, 128), BF16),
        ),
        in_specs=[SM, VM, VM, VM, VM, VM],
        out_specs=(VM, VM, VM, VM),
        scratch_shapes=[
            pltpu.VMEM((n + 4, 2, rows, feature), BF16),
            pltpu.VMEM((n, 2, rows, feature), BF16),
            pltpu.VMEM((4, 3, 2, rows, feature), BF16),
            dma((n,)),
            dma((n,)),
            dma((n,)),
            dma((n,)),
            dma((3, 4)),
            dma((3, 4)),
            dma,
            dma,
        ],
        compiler_params=pltpu.CompilerParams(collective_id=0, has_side_effects=True),
        name="fetch",
    )(
        cidx.reshape(-1),
        ask,
        k_blocks.reshape(blocks, 8, rows, feature),
        v_blocks.reshape(blocks, 8, rows, feature),
        q_blocks,
        do_blocks,
    )
    kv_list = kv_list.reshape(3, 2, length, feature)
    per_head = pl.BlockSpec((1, length, feature), lambda h, m: (h, 0, 0))
    own_block = pl.BlockSpec((1, length, feature), lambda h, m: (m[3], 0, 0))
    gq_mine, terms = pl.pallas_call(
        functools.partial(attend_kernel, scaling),
        out_shape=(heads_shape, jax.ShapeDtypeStruct((4, 2, length, feature), BF16)),
        grid_spec=pltpu.PrefetchScalarGridSpec(
            num_scalar_prefetch=1,
            grid=(4,),
            in_specs=[
                per_head,
                per_head,
                pl.BlockSpec((3, 2, length, feature), lambda h, m: (0, 0, 0, 0)),
                own_block,
                own_block,
            ],
            out_specs=[
                per_head,
                pl.BlockSpec((4, 2, length, feature), lambda h, m: (0, 0, 0, 0)),
            ],
            scratch_shapes=[
                pltpu.VMEM((4, length, length), F32),
                pltpu.VMEM((4, length, length), F32),
                pltpu.VMEM((4, 2, length, feature), F32),
                pltpu.VMEM((4, feature, length), BF16),
            ],
        ),
        compiler_params=pltpu.CompilerParams(vmem_limit_bytes=56 * 2**20),
        name="attend",
    )(meta, q_mine, do_mine, kv_list, k_blocks, v_blocks)
    part_shape = jax.ShapeDtypeStruct((blocks, 2, 4, rows, feature), BF16)
    gq, gk, gv = pl.pallas_call(
        functools.partial(return_kernel, n),
        out_shape=(heads_shape, part_shape, part_shape),
        in_specs=[SM, VM, VM, VM],
        out_specs=(VM, VM, VM),
        scratch_shapes=[
            pltpu.VMEM((4, 2, 4, rows, feature), BF16),
            pltpu.VMEM((4, 4, 2, rows, feature), BF16),
            pltpu.VMEM((4, 5, 2, rows, feature), BF16),
            pltpu.VMEM((n, 2, rows, feature), BF16),
            pltpu.VMEM((n, 2, rows, feature), BF16),
            pltpu.VMEM((4, 2, rows, feature), F32),
            pltpu.VMEM((2, 4, rows, feature), BF16),
            dma((n,)),
            dma((n,)),
            dma((4, 4)),
            dma((4, 4)),
            dma((3,)),
            dma((3,)),
        ],
        compiler_params=pltpu.CompilerParams(collective_id=1, has_side_effects=True),
        name="give_back",
    )(tix, terms.reshape(4, 2, 2, 4, rows, feature), gq_mine, asked)
    return (
        gq.reshape(queries.shape),
        gk.reshape(keys.shape),
        gv.reshape(values.shape),
    )


def solution(mesh):
    return jax.shard_map(
        body,
        mesh=mesh,
        in_specs=(
            P("ctx", "head", None),
            P("ctx", None),
            P("ctx", None),
            P("ctx", "head", None),
            P("ctx", None),
        ),
        out_specs=(P("ctx", "head", None), P("ctx", None), P("ctx", None)),
        check_vma=False,
    )
```

time: 743 us -> 132 us (0.18)
  the two profiles are of different devices: /device:TPU:1 before, /device:TPU:121 now
where the time goes in v1:
time: 132 us
  Pallas kernels  123 us (93%)
  local copies, waits for them, and re-layouts  7.06 us (5%)
    pallas_call x1, Pallas kernels, body(): pl.pallas_call(functools.partial(return_kernel, n), out_shape=(heads_shap...  62.6 us
    pallas_call x1, Pallas kernels, body(): pl.pallas_call(functools.partial(fetch_kernel, n), out_shape=(heads_shape...  40.3 us
    pallas_call x1, Pallas kernels, body(): pl.pallas_call(functools.partial(attend_kernel, scaling), out_shape=(head...  20 us
    unnamed x9, local copies, waits for them, and re-layouts  4.63 us

profile of v1, /device:TPU:121, one launch (start us, length us, event | category | flops | bytes accessed | tf_op | source)
XLA Modules:
  0.0 131.7 jit_solution(11030888171987174557)
XLA Ops:
  0.7 0.0 copy-start.2
  0.7 0.7 copy-done.2
  1.3 0.1 fusion.2
  1.4 0.6 reshape.56.cidx
  2.0 0.1 copy.11
  2.1 0.1 copy.9
  2.2 0.6 pad_add_fusion.1.meta
  2.8 0.1 copy.8
  2.9 0.1 select_reduce_fusion
  3.0 0.1 copy.10
  3.2 0.1 select_reduce_fusion.1
  3.3 0.1 pad_add_fusion
  3.3 0.6 reshape.55.tix
  4.0 0.8 broadcast_in_dim.78.ask
  4.7 40.3 %fetch.1 = (bf16[4,512,128]{2,1,0:T(8,128)(2,1)}, bf16[4,512,128]{2,1,0:T(8,128)(2,1)}, bf16[3,2,2,4,64,128]{5,4,3,2,1,0:T(8,128)(2,1)}, bf16[32,16,128]{2,1,0:T(8,128)(2,1)}) custom-call(s32[12]{0:T(128)} %reshape.56.cidx, bf16[32,16,128]{2,1,0:T(8,128)(2,1)} %broadcast_in_dim.78.ask, bf16[4,8,64,128]{3,2,1,0:T(8,128)(2,1)} %bitcast.14, ...), custom_call_target="tpu_custom_call" | custom-call | tf_op jit(solution)/shard_map/fetch/pallas_call | solution.py:431
  45.1 20.0 %attend.1 = (bf16[4,512,128]{2,1,0:T(8,128)(2,1)}, bf16[4,2,512,128]{3,2,1,0:T(8,128)(2,1)}) custom-call(s32[4]{0:T(128)} %pad_add_fusion.1.meta, bf16[4,512,128]{2,1,0:T(8,128)(2,1)} %get-tuple-element.12.q_ref, bf16[4,512,128]{2,1,0:T(8,128)(2,1)} %get-tuple-element.13.do_ref, bf16[3,2,512,128]{3,2,1,0:T(8,128)(2,1)} %bitcast.19, ...), custom_call_target="tpu_custom_call" | custom-call | tf_op jit(solution)/shard_map/attend/pallas_call | solution.py:467
  65.1 62.6 %give_back.1 = (bf16[4,512,128]{2,1,0:T(8,128)(2,1)}, bf16[4,2,4,64,128]{4,3,2,1,0:T(8,128)(2,1)}, bf16[4,2,4,64,128]{4,3,2,1,0:T(8,128)(2,1)}) custom-call(s32[144]{0:T(256)} %reshape.55.tix, bf16[4,2,2,4,64,128]{5,4,3,2,1,0:T(8,128)(2,1)} %bitcast.18, bf16[4,512,128]{2,1,0:T(8,128)(2,1)} %get-tuple-element.16.gq, bf16[32,16,128]{2,1,0:T(8,128)(2,1)} %get-tuple-element.17.asked), custom_call_target="tpu_custom_call" | custom-call | tf_op jit(solution)/shard_map/give_back/pallas_call | solution.py:495
  127.7 0.0 copy-start.1
  127.7 1.9 %copy.16 = bf16[2048,1,128]{2,0,1:T(8,128)(2,1)} copy(bf16[2048,1,128]{2,0,1:T(8,128)(2,1)} %bitcast.24) | data formatting | bytes 1048576
  129.6 0.0 copy-done.1
  129.6 0.0 copy-start
  129.6 0.8 copy.17
  130.4 0.4 copy-done
  130.9 0.8 copy.18
  (5 shorter events, 0.0 us)
Async XLA Ops:
  0.7 0.7 copy-start.2
  127.7 1.9 %copy-start.1 = (bf16[4,2,4,64,128]{4,3,2,1,0:T(8,128)(2,1)S(1)}, bf16[4,2,4,64,128]{4,3,2,1,0:T(8,128)(2,1)}, u32[]{:S(2)}) copy-start(bf16[4,2,4,64,128]{4,3,2,1,0:T(8,128)(2,1)} %get-tuple-element.19) | copy-start | bytes 1572868
  129.6 1.2 copy-start

commit v2 on v1

--- a/solution.py
+++ b/solution.py
@@ -15,35 +15,31 @@
 SM = pl.BlockSpec(memory_space=pltpu.SMEM)
 
 
-def greet(n):
+def place():
     me = lax.axis_index("ctx")
     head = lax.axis_index("head")
-    chip, core = head // 2, head % 2
+    return me // 4, me % 4, head // 2, head % 2
+
+
+def greet(nz):
+    z, y, chip, core = place()
     barrier = pltpu.get_barrier_semaphore()
 
-    def hello(step, carry):
-        pl.semaphore_signal(
-            barrier, inc=1, device_id={"ctx": lax.rem(me + step, n)}, device_id_type=MESH
-        )
-        return carry
-
-    lax.fori_loop(1, n, hello, 0)
+    def hello(**where):
+        pl.semaphore_signal(barrier, inc=1, device_id=where, device_id_type=MESH)
+
+    hello(ctx=lax.rem(z + 1, nz) * 4 + y)
+    hello(ctx=lax.rem(z + nz - 1, nz) * 4 + y)
     for step in range(1, 4):
-        pl.semaphore_signal(
-            barrier,
-            inc=1,
-            device_id={"head": lax.rem(chip + step, 4) * 2 + core},
-            device_id_type=MESH,
-        )
-    pl.semaphore_signal(
-        barrier, inc=1, device_id={"head": chip * 2 + 1 - core}, device_id_type=MESH
-    )
-    pl.semaphore_wait(barrier, n - 1 + 4)
-    return me, chip, core
+        hello(ctx=z * 4 + lax.rem(y + step, 4))
+        hello(head=lax.rem(chip + step, 4) * 2 + core)
+    hello(head=chip * 2 + 1 - core)
+    pl.semaphore_wait(barrier, 9)
+    return z, y, chip, core
 
 
 def fetch_kernel(
-    n,
+    nz,
     cidx,
     ask,
     keys,
@@ -54,20 +50,25 @@
     do_out,
     kv_out,
     asked,
-    table,
+    pool,
     send,
     comp,
     ask_send,
     ask_recv,
-    kv_send,
-    kv_recv,
+    z_send,
+    z_recv,
+    y_send,
+    y_recv,
     x_send,
     x_recv,
     core_send,
     core_recv,
 ):
     rows = keys.shape[2]
-    me, chip, core = greet(n)
+    reach = nz // 2
+    wrap = nz - 1 - reach
+    z, y, chip, core = greet(nz)
+    part = core * 4 + chip
 
     def to_chip(step, slot, src, dst):
         peer = lax.rem(chip + step, 4)
@@ -80,69 +81,134 @@
             device_id_type=MESH,
         )
 
-    def ask_copy(owner, place):
+    def ask_copy(step):
+        peer = lax.rem(y + step, 4)
         return pltpu.make_async_remote_copy(
-            src_ref=ask.at[owner],
-            dst_ref=asked.at[place],
-            send_sem=ask_send.at[owner],
-            recv_sem=ask_recv.at[place],
-            device_id={"ctx": owner},
+            src_ref=ask.at[peer],
+            dst_ref=asked.at[y],
+            send_sem=ask_send.at[step],
+            recv_sem=ask_recv.at[step],
+            device_id={"ctx": z * 4 + peer},
             device_id_type=MESH,
         )
 
-    def kv_copy(reader, place):
+    def relay(source, half, back, hop):
+        there = pool.at[pl.ds(4 * source, 4), half]
+        if hop == 1:
+            here = (keys, values)[half].at[:, part]
+        else:
+            here = there
+        peer = lax.rem(z + nz - 1, nz) if back else lax.rem(z + 1, nz)
         return pltpu.make_async_remote_copy(
-            src_ref=send.at[reader],
-            dst_ref=table.at[place],
-            send_sem=kv_send.at[reader],
-            recv_sem=kv_recv.at[place],
-            device_id={"ctx": reader},
+            src_ref=here,
+            dst_ref=there,
+            send_sem=z_send.at[back, hop - 1, half],
+            recv_sem=z_recv.at[source, half],
+            device_id={"ctx": peer * 4 + y},
             device_id_type=MESH,
         )
 
-    def start_ask(owner, carry):
-        ask_copy(owner, me).start()
-        return carry
-
-    lax.fori_loop(0, me, start_ask, 0)
+    def forward_source(hop):
+        return z - hop + 1, jnp.logical_and(z <= nz - 2, z >= hop - 1)
+
+    def backward_source(hop):
+        source = lax.rem(z + hop - 1, nz)
+        return source, source <= wrap - 1
+
+    def start_relay(back, hop, half):
+        source, needed = (backward_source if back else forward_source)(hop)
+
+        @pl.when(needed)
+        def _():
+            relay(source, half, back, hop).start()
+
+    def slot_copy(step, source):
+        peer = lax.rem(y + step, 4)
+        return pltpu.make_async_remote_copy(
+            src_ref=send.at[step - 1, source],
+            dst_ref=pool.at[4 * nz + 4 * source + y],
+            send_sem=y_send.at[step - 1, source],
+            recv_sem=y_recv.at[step - 1, source],
+            device_id={"ctx": z * 4 + peer},
+            device_id_type=MESH,
+        )
+
+    def serve(source):
+        for step in range(1, 4):
+            peer = lax.rem(y + step, 4)
+            wish = jnp.broadcast_to(asked[peer, pl.ds(source, 1)], (16, 128))
+            masks = [jnp.where(wish == b, 1.0, 0.0).astype(BF16) for b in range(4)]
+            for half in range(2):
+                for g in range(rows // 16):
+                    span = pl.ds(16 * g, 16)
+                    total = pool[4 * source, half, span] * masks[0]
+                    for b in range(1, 4):
+                        total = total + pool[4 * source + b, half, span] * masks[b]
+                    send[step - 1, source, half, span] = total
+        for step in range(1, 4):
+            slot_copy(step, source).start()
+
+    asks = [ask_copy(step) for step in range(1, 4)]
+    for copy in asks:
+        copy.start()
+    for half in range(2):
+        start_relay(0, 1, half)
+        start_relay(1, 1, half)
     q_copies = []
     for step in (1, 3, 2):
         q_copies.append(to_chip(step, 0, lambda peer: queries.at[peer], q_out.at[chip]))
         q_copies.append(to_chip(step, 1, lambda peer: dout.at[peer], do_out.at[chip]))
     for copy in q_copies:
         copy.start()
+    for b in range(4):
+        pool[4 * z + b, 0] = keys[b, part]
+        pool[4 * z + b, 1] = values[b, part]
+    asked[y] = ask[y]
+    for copy in asks:
+        copy.wait_recv()
+    serve(z)
     q_out[chip] = queries[chip]
     do_out[chip] = dout[chip]
-    part = core * 4 + chip
-    for b in range(4):
-        table[n + b, 0] = keys[b, part]
-        table[n + b, 1] = values[b, part]
-
-    def serve(reader, carry):
-        ask_copy(reader, reader).wait_recv()
-        wish = asked[reader].astype(F32)
-        masks = [jnp.where(wish == b, 1.0, 0.0).astype(BF16) for b in range(4)]
+    for hop in range(1, reach + 1):
+        near = z - hop
+        far = lax.rem(z + hop, nz)
         for half in range(2):
-            for g in range(rows // 16):
-                span = pl.ds(16 * g, 16)
-                total = table[n, half, span] * masks[0]
-                for b in range(1, 4):
-                    total = total + table[n + b, half, span] * masks[b]
-                send[reader, half, span] = total
-        kv_copy(reader, me).start()
+
+            @pl.when(near >= 0)
+            def _():
+                relay(near, half, 0, 2).wait_recv()
+
+            if hop < reach:
+                start_relay(0, hop + 1, half)
+            if hop <= wrap:
+
+                @pl.when(far <= wrap - 1)
+                def _():
+                    relay(far, half, 1, 2).wait_recv()
+
+                if hop < wrap:
+                    start_relay(1, hop + 1, half)
+
+        @pl.when(near >= 0)
+        def _():
+            serve(near)
+
+        if hop <= wrap:
+
+            @pl.when(jnp.logical_and(far <= wrap - 1, far < z))
+            def _():
+                serve(far)
+
+    def got_slots(source, carry):
+        for step in range(1, 4):
+            slot_copy(step, source).wait_recv()
         return carry
 
-    lax.fori_loop(me + 1, n, serve, 0)
-
-    def got_kv(owner, carry):
-        kv_copy(owner, owner).wait_recv()
-        return carry
-
-    lax.fori_loop(0, me, got_kv, 0)
+    lax.fori_loop(0, z + 1, got_slots, 0)
 
     for x in range(4):
         for t in range(3):
-            comp[x, t] = table[cidx[x * 3 + t]]
+            comp[x, t] = pool[cidx[x * 3 + t]]
     kv_copies = [
         to_chip(step, 2, lambda peer: comp.at[peer], kv_out.at[:, :, core, chip])
         for step in (1, 3, 2)
@@ -165,20 +231,23 @@
     swap.start()
     for copy in q_copies:
         copy.wait()
-    for copy in kv_copies:
+    for copy in kv_copies + asks:
         copy.wait_send()
-
-    def sent_ask(owner, carry):
-        ask_copy(owner, me).wait_send()
+    for back, last in ((0, reach), (1, wrap)):
+        for hop in range(1, last + 1):
+            source, needed = (backward_source if back else forward_source)(hop)
+            for half in range(2):
+
+                @pl.when(needed)
+                def _():
+                    relay(source, half, back, hop).wait_send()
+
+    def sent_slots(source, carry):
+        for step in range(1, 4):
+            slot_copy(step, source).wait_send()
         return carry
 
-    lax.fori_loop(0, me, sent_ask, 0)
-
-    def sent_kv(reader, carry):
-        kv_copy(reader, me).wait_send()
-        return carry
-
-    lax.fori_loop(me + 1, n, sent_kv, 0)
+    lax.fori_loop(0, z + 1, sent_slots, 0)
     swap.wait()
 
 
@@ -247,7 +316,7 @@
 
 
 def return_kernel(
-    n,
+    nz,
     tix,
     terms,
     gq,
@@ -258,19 +327,26 @@
     pair,
     outgoing,
     incoming,
-    send,
-    back,
-    own,
+    y_out,
+    y_in,
+    sums,
+    z_out,
+    z_in,
     final,
-    back_send,
-    back_recv,
+    y_send,
+    y_recv,
+    z_send,
+    z_recv,
     x_send,
     x_recv,
     core_send,
     core_recv,
 ):
     rows = terms.shape[4]
-    me, chip, core = greet(n)
+    n = 4 * nz
+    reach = nz // 2
+    wrap = nz - 1 - reach
+    z, y, chip, core = greet(nz)
 
     def to_chip(step, slot, src, dst):
         peer = lax.rem(chip + step, 4)
@@ -293,13 +369,24 @@
             device_id_type=MESH,
         )
 
-    def back_copy(owner, place):
+    def slot_copy(step, owner):
         return pltpu.make_async_remote_copy(
-            src_ref=send.at[owner],
-            dst_ref=back.at[place],
-            send_sem=back_send.at[owner],
-            recv_sem=back_recv.at[place],
-            device_id={"ctx": owner},
+            src_ref=y_out.at[step, owner],
+            dst_ref=y_in.at[step, owner],
+            send_sem=y_send.at[step, owner],
+            recv_sem=y_recv.at[step, owner],
+            device_id={"ctx": z * 4 + lax.rem(y + step, 4)},
+            device_id_type=MESH,
+        )
+
+    def relay(owner, half, back):
+        peer = lax.rem(z + 1, nz) if back else lax.rem(z + nz - 1, nz)
+        return pltpu.make_async_remote_copy(
+            src_ref=z_out.at[owner, half],
+            dst_ref=z_in.at[back, owner, half],
+            send_sem=z_send.at[owner, half],
+            recv_sem=z_recv.at[back, owner, half],
+            device_id={"ctx": peer * 4 + y},
             device_id_type=MESH,
         )
 
@@ -307,6 +394,8 @@
     merge.start()
     for x in range(4):
         incoming[x, 4] = jnp.zeros_like(incoming[x, 4])
+    for owner in range(nz):
+        sums[owner] = jnp.zeros_like(sums[owner])
     merge.wait()
     for t in range(4):
         for half in range(2):
@@ -333,34 +422,101 @@
             total = total + incoming[x, tix[x * (n + 4) + place]].astype(F32)
         return total
 
-    def give_back(owner, carry):
-        send[owner] = collect(owner).astype(BF16)
-        back_copy(owner, me).start()
-        return carry
-
-    lax.fori_loop(0, me, give_back, 0)
+    def give(owner):
+        for step in range(4):
+            y_out[step, owner] = collect(4 * owner + lax.rem(y + step, 4)).astype(BF16)
+        for step in range(1, 4):
+            slot_copy(step, owner).start()
+
+    def gather(owner):
+        for step in range(1, 4):
+            slot_copy(step, owner).wait_recv()
+        masks = []
+        for step in range(4):
+            wish = jnp.broadcast_to(asked[lax.rem(y + 4 - step, 4), pl.ds(owner, 1)], (16, 128))
+            masks.append([jnp.where(wish == b, 1.0, 0.0) for b in range(4)])
+        for half in range(2):
+            for g in range(rows // 16):
+                span = pl.ds(16 * g, 16)
+                parts = [y_out[0, owner, half, span].astype(F32)]
+                for step in range(1, 4):
+                    parts.append(y_in[step, owner, half, span].astype(F32))
+                for b in range(4):
+                    total = parts[0] * masks[0][b]
+                    for step in range(1, 4):
+                        total = total + parts[step] * masks[step][b]
+                    sums[owner, half, b, span] = total
+
+    def pass_on(owner, half, back, last):
+        if last:
+            z_out[owner, half] = sums[owner, half].astype(BF16)
+        elif back:
+            relay(owner, half, back).wait_recv()
+            z_out[owner, half] = (
+                sums[owner, half] + z_in[back, owner, half].astype(F32)
+            ).astype(BF16)
+        else:
+
+            @pl.when(z <= nz - 2)
+            def _():
+                relay(owner, half, back).wait_recv()
+                z_out[owner, half] = (
+                    sums[owner, half] + z_in[back, owner, half].astype(F32)
+                ).astype(BF16)
+
+            @pl.when(z == nz - 1)
+            def _():
+                z_out[owner, half] = sums[owner, half].astype(BF16)
+
+        relay(owner, half, back).start()
+
+    steps = []
+    for i in range(reach):
+        near = z - (reach - i)
+        steps.append((near, near >= 0, near >= 0, 0, i == 0))
+        if i < wrap:
+            far = lax.rem(z + wrap - i, nz)
+            needed = far <= wrap - 1
+            steps.append((far, needed, jnp.logical_and(needed, far < z), 1, i == 0))
+    for owner, _, mine, _, _ in steps:
+
+        @pl.when(mine)
+        def _():
+            give(owner)
+
+    give(z)
     for copy in gq_copies:
         copy.start()
     gq_out[chip] = gq[chip]
+    for owner, needed, mine, back, last in steps:
+
+        @pl.when(mine)
+        def _():
+            gather(owner)
+
+        @pl.when(needed)
+        def _():
+            for half in range(2):
+                pass_on(owner, half, back, last)
+
+    gather(z)
     for b in range(4):
-        own[b] = collect(n + b)
-
-    def take_back(reader, carry):
-        back_copy(reader, reader).wait_recv()
-        wish = asked[reader].astype(F32)
-        masks = [jnp.where(wish == b, 1.0, 0.0) for b in range(4)]
+        near_sum = collect(n + b)
         for half in range(2):
-            for g in range(rows // 16):
-                span = pl.ds(16 * g, 16)
-                part = back[reader, half, span].astype(F32)
-                for b in range(4):
-                    own[b, half, span] += part * masks[b]
-        return carry
-
-    lax.fori_loop(me + 1, n, take_back, 0)
-    for b in range(4):
-        final[0, b] = own[b, 0].astype(BF16)
-        final[1, b] = own[b, 1].astype(BF16)
+            sums[z, half, b] += near_sum[half]
+    for half in range(2):
+
+        @pl.when(z <= nz - 2)
+        def _():
+            relay(z, half, 0).wait_recv()
+            sums[z, half] += z_in[0, z, half].astype(F32)
+
+        @pl.when(z <= wrap - 1)
+        def _():
+            relay(z, half, 1).wait_recv()
+            sums[z, half] += z_in[1, z, half].astype(F32)
+
+        final[half] = sums[z, half].astype(BF16)
     shares = []
     for step in (1, 3, 2):
         shares.append(to_chip(step, 2, lambda peer: final.at[0], gk_out.at[:, core, chip]))
@@ -380,12 +536,19 @@
         copy.wait_send()
     for copy in gq_copies:
         copy.wait()
-
-    def sent_back(owner, carry):
-        back_copy(owner, me).wait_send()
+    for owner, needed, _, back, _ in steps:
+
+        @pl.when(needed)
+        def _():
+            for half in range(2):
+                relay(owner, half, back).wait_send()
+
+    def sent_slots(owner, carry):
+        for step in range(1, 4):
+            slot_copy(step, owner).wait_send()
         return carry
 
-    lax.fori_loop(0, me, sent_back, 0)
+    lax.fori_loop(0, z + 1, sent_slots, 0)
     swap_k.wait()
     swap_v.wait()
 
@@ -410,8 +573,11 @@
     peers = jnp.arange(n, dtype=jnp.int32)
     hits = distant[:, :, None] & (owners[:, :, None] == peers)
     wanted = jnp.max(jnp.where(hits, inside[:, :, None], -1), axis=(0, 1))
-    ask = jnp.broadcast_to(wanted.astype(BF16)[:, None, None], (n, 16, 128))
-    cidx = jnp.where(vacant, n + local[:, None], jnp.where(owners == me, n + inside, owners))
+    nz = n // 4
+    ask = jnp.broadcast_to(wanted.astype(F32).reshape(nz, 4).T[:, :, None], (4, nz, 128))
+    column = owners % 4 == me % 4
+    cidx = jnp.where(column, owners // 4 * 4 + inside, n + owners)
+    cidx = jnp.where(vacant, me // 4 * 4 + local[:, None], cidx)
     near_hits = near[:, :, None] & (inside[:, :, None] == local)
     tcol = jnp.arange(3, dtype=jnp.int32)[None, :, None]
     far_t = jnp.min(jnp.where(hits, tcol, 4), axis=1)
@@ -429,23 +595,25 @@
     v_blocks = values.reshape(blocks, length, feature)
     heads_shape = jax.ShapeDtypeStruct((4, length, feature), BF16)
     q_mine, do_mine, kv_list, asked = pl.pallas_call(
-        functools.partial(fetch_kernel, n),
+        functools.partial(fetch_kernel, nz),
         out_shape=(
             heads_shape,
             heads_shape,
             jax.ShapeDtypeStruct((3, 2, 2, 4, rows, feature), BF16),
-            jax.ShapeDtypeStruct((n, 16, 128), BF16),
+            jax.ShapeDtypeStruct((4, nz, 128), F32),
         ),
         in_specs=[SM, VM, VM, VM, VM, VM],
         out_specs=(VM, VM, VM, VM),
         scratch_shapes=[
-            pltpu.VMEM((n + 4, 2, rows, feature), BF16),
-            pltpu.VMEM((n, 2, rows, feature), BF16),
+            pltpu.VMEM((2 * n, 2, rows, feature), BF16),
+            pltpu.VMEM((3, nz, 2, rows, feature), BF16),
             pltpu.VMEM((4, 3, 2, rows, feature), BF16),
-            dma((n,)),
-            dma((n,)),
-            dma((n,)),
-            dma((n,)),
+            dma((4,)),
+            dma((4,)),
+            dma((2, nz // 2, 2)),
+            dma((nz, 2)),
+            dma((3, nz)),
+            dma((3, nz)),
             dma((3, 4)),
             dma((3, 4)),
             dma,
@@ -493,7 +661,7 @@
     )(meta, q_mine, do_mine, kv_list, k_blocks, v_blocks)
     part_shape = jax.ShapeDtypeStruct((blocks, 2, 4, rows, feature), BF16)
     gq, gk, gv = pl.pallas_call(
-        functools.partial(return_kernel, n),
+        functools.partial(return_kernel, nz),
         out_shape=(heads_shape, part_shape, part_shape),
         in_specs=[SM, VM, VM, VM],
         out_specs=(VM, VM, VM),
@@ -501,12 +669,16 @@
             pltpu.VMEM((4, 2, 4, rows, feature), BF16),
             pltpu.VMEM((4, 4, 2, rows, feature), BF16),
             pltpu.VMEM((4, 5, 2, rows, feature), BF16),
-            pltpu.VMEM((n, 2, rows, feature), BF16),
-            pltpu.VMEM((n, 2, rows, feature), BF16),
-            pltpu.VMEM((4, 2, rows, feature), F32),
+            pltpu.VMEM((4, nz, 2, rows, feature), BF16),
+            pltpu.VMEM((4, nz, 2, rows, feature), BF16),
+            pltpu.VMEM((nz, 2, 4, rows, feature), F32),
+            pltpu.VMEM((nz, 2, 4, rows, feature), BF16),
+            pltpu.VMEM((2, nz, 2, 4, rows, feature), BF16),
             pltpu.VMEM((2, 4, rows, feature), BF16),
-            dma((n,)),
-            dma((n,)),
+            dma((4, nz)),
+            dma((4, nz)),
+            dma((nz, 2)),
+            dma((2, nz, 2)),
             dma((4, 4)),
             dma((4, 4)),
             dma((3,)),

time: 132 us -> 113 us (0.86)
  the two profiles are of different devices: /device:TPU:121 before, /device:TPU:1 now
where the time goes in v2:
time: 113 us
  Pallas kernels  104 us (92%)
  local copies, waits for them, and re-layouts  7.15 us (6%)
    pallas_call x1, Pallas kernels, body(): pl.pallas_call(functools.partial(return_kernel, nz), out_shape=(heads_sha...  53 us
    pallas_call x1, Pallas kernels, body(): pl.pallas_call(functools.partial(fetch_kernel, nz), out_shape=(heads_shap...  31.4 us
    pallas_call x1, Pallas kernels, body(): pl.pallas_call(functools.partial(attend_kernel, scaling), out_shape=(head...  20 us
    unnamed x9, local copies, waits for them, and re-layouts  4.63 us

profile of v2, /device:TPU:1, one launch (start us, length us, event | category | flops | bytes accessed | tf_op | source)
XLA Modules:
  0.0 113.2 jit_solution(6380165854987296859)
XLA Ops:
  0.7 0.0 copy-start.2
  0.7 0.7 copy-done.2
  1.4 0.1 fusion.6
  1.4 0.6 reshape.57.cidx
  2.1 0.1 copy.13
  2.2 0.1 copy.11
  2.3 0.6 pad_add_fusion.1.meta
  2.9 0.1 copy.10
  3.0 0.1 select_reduce_fusion
  3.1 0.1 copy.12
  3.2 0.1 select_reduce_fusion.1
  3.3 0.1 pad_add_fusion
  3.3 0.6 reshape.56.tix
  4.0 0.1 convert_element_type.12
  4.1 0.1 copy.15
  4.2 0.7 broadcast_in_dim.78.ask
  4.8 31.4 %fetch.1 = (bf16[4,512,128]{2,1,0:T(8,128)(2,1)}, bf16[4,512,128]{2,1,0:T(8,128)(2,1)}, bf16[3,2,2,4,64,128]{5,4,3,2,1,0:T(8,128)(2,1)}, f32[4,8,128]{2,1,0:T(8,128)}) custom-call(s32[12]{0:T(128)} %reshape.57.cidx, f32[4,8,128]{2,1,0:T(8,128)} %broadcast_in_dim.78.ask, bf16[4,8,64,128]{3,2,1,0:T(8,128)(2,1)} %bitcast.15, bf16[4,8,64,128]{3,2,1,0:T(8,128)(2,1)} %bitcast.17, ...), custom_call_target="tpu_custom_call" | custom-call | tf_op jit(solution)/shard_map/fetch/pallas_call | solution.py:597
  36.2 20.0 %attend.1 = (bf16[4,512,128]{2,1,0:T(8,128)(2,1)}, bf16[4,2,512,128]{3,2,1,0:T(8,128)(2,1)}) custom-call(s32[4]{0:T(128)} %pad_add_fusion.1.meta, bf16[4,512,128]{2,1,0:T(8,128)(2,1)} %get-tuple-element.12.q_ref, bf16[4,512,128]{2,1,0:T(8,128)(2,1)} %get-tuple-element.13.do_ref, bf16[3,2,512,128]{3,2,1,0:T(8,128)(2,1)} %bitcast.20, ...), custom_call_target="tpu_custom_call" | custom-call | tf_op jit(solution)/shard_map/attend/pallas_call | solution.py:635
  56.2 53.0 %give_back.1 = (bf16[4,512,128]{2,1,0:T(8,128)(2,1)}, bf16[4,2,4,64,128]{4,3,2,1,0:T(8,128)(2,1)}, bf16[4,2,4,64,128]{4,3,2,1,0:T(8,128)(2,1)}) custom-call(s32[144]{0:T(256)} %reshape.56.tix, bf16[4,2,2,4,64,128]{5,4,3,2,1,0:T(8,128)(2,1)} %bitcast.19, bf16[4,512,128]{2,1,0:T(8,128)(2,1)} %get-tuple-element.16.gq, f32[4,8,128]{2,1,0:T(8,128)} %get-tuple-element.17.asked), custom_call_target="tpu_custom_call" | custom-call | tf_op jit(solution)/shard_map/give_back/pallas_call | solution.py:663
  109.2 0.0 copy-start.1
  109.2 1.9 %copy.19 = bf16[2048,1,128]{2,0,1:T(8,128)(2,1)} copy(bf16[2048,1,128]{2,0,1:T(8,128)(2,1)} %bitcast.25) | data formatting | bytes 1048576
  111.2 0.0 copy-done.1
  111.2 0.0 copy-start
  111.2 0.8 copy.20
  112.0 0.4 copy-done
  112.4 0.8 copy.21
  (5 shorter events, 0.0 us)
Async XLA Ops:
  0.7 0.7 copy-start.2
  109.2 1.9 %copy-start.1 = (bf16[4,2,4,64,128]{4,3,2,1,0:T(8,128)(2,1)S(1)}, bf16[4,2,4,64,128]{4,3,2,1,0:T(8,128)(2,1)}, u32[]{:S(2)}) copy-start(bf16[4,2,4,64,128]{4,3,2,1,0:T(8,128)(2,1)} %get-tuple-element.19) | copy-start | bytes 1572868
  111.2 1.2 %copy-start = (bf16[4,2,4,64,128]{4,3,2,1,0:T(8,128)(2,1)S(1)}, bf16[4,2,4,64,128]{4,3,2,1,0:T(8,128)(2,1)}, u32[]{:S(2)}) copy-start(bf16[4,2,4,64,128]{4,3,2,1,0:T(8,128)(2,1)} %get-tuple-element.20) | copy-start | bytes 1572868

commit v3 on v2

v3 whole, which is shorter than its diff:
```python
import functools
import math

import jax
import jax.numpy as jnp
from jax import lax
from jax.experimental import pallas as pl
from jax.experimental.pallas import tpu as pltpu
from jax.sharding import PartitionSpec as P

MESH = pl.DeviceIdType.MESH
F32 = jnp.float32
BF16 = jnp.bfloat16
VM = pl.BlockSpec(memory_space=pltpu.VMEM)
SM = pl.BlockSpec(memory_space=pltpu.SMEM)


def place():
    me = lax.axis_index("ctx")
    head = lax.axis_index("head")
    return me // 4, me % 4, head // 2, head % 2


def greet(nz):
    z, y, chip, core = place()
    barrier = pltpu.get_barrier_semaphore()

    def hello(**where):
        pl.semaphore_signal(barrier, inc=1, device_id=where, device_id_type=MESH)

    hello(ctx=lax.rem(z + 1, nz) * 4 + y)
    hello(ctx=lax.rem(z + nz - 1, nz) * 4 + y)
    for step in range(1, 4):
        hello(ctx=z * 4 + lax.rem(y + step, 4))
        hello(head=lax.rem(chip + step, 4) * 2 + core)
    hello(head=chip * 2 + 1 - core)
    pl.semaphore_wait(barrier, 9)
    return z, y, chip, core


def kernel(
    nz,
    scaling,
    selected,
    keys,
    values,
    queries,
    dout,
    gq_out,
    gk_out,
    gv_out,
    ask,
    asked,
    pool,
    send,
    comp,
    near_kv,
    qs,
    dos,
    expo,
    dprobs,
    own_stats,
    stats,
    turned,
    gq_sum,
    gqs,
    terms,
    pair,
    outgoing,
    incoming,
    own_in,
    y_out,
    y_in,
    sums,
    z_out,
    z_in,
    final,
    ask_send,
    ask_recv,
    z_send,
    z_recv,
    y_send,
    y_recv,
    x_send,
    x_recv,
    core_send,
    core_recv,
    back_y_send,
    back_y_recv,
    back_z_send,
    back_z_recv,
):
    rows, feature = keys.shape[2:]
    length = 8 * rows
    n = 4 * nz
    reach = nz // 2
    wrap = nz - 1 - reach
    factor = scaling * math.log2(math.e)
    nt = (((1,), (1,)), ((), ()))
    z, y, chip, core = place()
    me = 4 * z + y
    part = core * 4 + chip

    cidx, code, tiles = [], [], [None] * 4
    spot = 4 * lax.broadcasted_iota(jnp.int32, (nz, 128), 0)
    for x in range(4):
        for t in range(3):
            named = selected[x, t]
            owner = lax.div(named, 4)
            inside = named - 4 * owner
            vacant = named == 4 * me + x
            plane = lax.div(owner, 4)
            seat = jnp.where(owner - 4 * plane == y, 4 * plane + inside, n + owner)
            cidx.append(jnp.where(vacant, 4 * z + x, seat))
            code.append(jnp.where(vacant, -1, jnp.where(owner == me, n + inside, owner)))
            for peer in range(4):
                tile = jnp.where(spot + peer == code[-1], inside, -1)
                tiles[peer] = tile if tiles[peer] is None else jnp.maximum(tiles[peer], tile)
    for peer in range(4):
        ask[peer] = tiles[peer].astype(F32)
    for b in range(4):
        pool[4 * z + b, 0] = keys[b, part]
        pool[4 * z + b, 1] = values[b, part]
    greet(nz)

    def to_chip(step, slot, src, dst):
        peer = lax.rem(chip + step, 4)
        return pltpu.make_async_remote_copy(
            src_ref=src(peer),
            dst_ref=dst,
            send_sem=x_send.at[slot, step],
            recv_sem=x_recv.at[slot, step],
            device_id={"head": peer * 2 + core},
            device_id_type=MESH,
        )

    def to_core(slot, src, dst):
        return pltpu.make_async_remote_copy(
            src_ref=src,
            dst_ref=dst,
            send_sem=core_send.at[slot],
            recv_sem=core_recv.at[slot],
            device_id={"head": chip * 2 + 1 - core},
            device_id_type=MESH,
        )

    def ask_copy(step):
        peer = lax.rem(y + step, 4)
        return pltpu.make_async_remote_copy(
            src_ref=ask.at[peer],
            dst_ref=asked.at[y],
            send_sem=ask_send.at[step],
            recv_sem=ask_recv.at[step],
            device_id={"ctx": z * 4 + peer},
            device_id_type=MESH,
        )

    def relay(source, half, back, hop):
        there = pool.at[pl.ds(4 * source, 4), half]
        if hop == 1:
            here = (keys, values)[half].at[:, part]
        else:
            here = there
        peer = lax.rem(z + nz - 1, nz) if back else lax.rem(z + 1, nz)
        return pltpu.make_async_remote_copy(
            src_ref=here,
            dst_ref=there,
            send_sem=z_send.at[back, hop - 1, half],
            recv_sem=z_recv.at[source, half],
            device_id={"ctx": peer * 4 + y},
            device_id_type=MESH,
        )

    def forward_source(hop):
        return z - hop + 1, jnp.logical_and(z <= nz - 2, z >= hop - 1)

    def backward_source(hop):
        source = lax.rem(z + hop - 1, nz)
        return source, source <= wrap - 1

    def start_relay(back, hop, half):
        source, needed = (backward_source if back else forward_source)(hop)

        @pl.when(needed)
        def _():
            relay(source, half, back, hop).start()

    def slot_copy(step, source):
        peer = lax.rem(y + step, 4)
        return pltpu.make_async_remote_copy(
            src_ref=send.at[step - 1, source],
            dst_ref=pool.at[4 * nz + 4 * source + y],
            send_sem=y_send.at[step - 1, source],
            recv_sem=y_recv.at[step - 1, source],
            device_id={"ctx": z * 4 + peer},
            device_id_type=MESH,
        )

    def serve(source):
        for step in range(1, 4):
            peer = lax.rem(y + step, 4)
            wish = jnp.broadcast_to(asked[peer, pl.ds(source, 1)], (16, 128))
            masks = [jnp.where(wish == b, 1.0, 0.0).astype(BF16) for b in range(4)]
            for half in range(2):
                for g in range(rows // 16):
                    span = pl.ds(16 * g, 16)
                    total = pool[4 * source, half, span] * masks[0]
                    for b in range(1, 4):
                        total = total + pool[4 * source + b, half, span] * masks[b]
                    send[step - 1, source, half, span] = total
        for step in range(1, 4):
            slot_copy(step, source).start()

    def key_rows(t):
        block = near_kv[t, 0] if t < 3 else keys[chip]
        return block.reshape(length, feature)

    def value_rows(t):
        block = near_kv[t, 1] if t < 3 else values[chip]
        return block.reshape(length, feature)

    def attend_own(h):
        s = lax.dot_general(key_rows(3), qs[h], nt, preferred_element_type=F32)
        col = lax.broadcasted_iota(jnp.int32, (length, length), 0)
        row = lax.broadcasted_iota(jnp.int32, (length, length), 1)
        s = jnp.where(col <= row, s, -jnp.inf)
        top = jnp.max(s, axis=0, keepdims=True) * factor
        e = jnp.exp2(s * factor - top)
        dp = lax.dot_general(value_rows(3), dos[h], nt, preferred_element_type=F32)
        expo[h, 3] = e
        dprobs[h, 3] = dp
        own_stats[h, 0] = top
        own_stats[h, 1] = jnp.sum(e, axis=0, keepdims=True)
        own_stats[h, 2] = jnp.sum(e * dp, axis=0, keepdims=True)

    live = [selected[chip, t] != 4 * me + chip for t in range(3)]

    def attend_far(h):
        q, do = qs[h], dos[h]
        top = own_stats[h, 0]
        for t in range(3):
            s = lax.dot_general(key_rows(t), q, nt, preferred_element_type=F32)
            expo[h, t] = s
            best = jnp.max(s, axis=0, keepdims=True) * factor
            top = jnp.maximum(top, jnp.where(live[t], best, -jnp.inf))
        shrink = jnp.exp2(own_stats[h, 0] - top)
        total = own_stats[h, 1] * shrink
        weighted = own_stats[h, 2] * shrink
        for t in range(3):
            e = jnp.exp2(expo[h, t] * factor - jnp.where(live[t], top, jnp.inf))
            dp = lax.dot_general(value_rows(t), do, nt, preferred_element_type=F32)
            total = total + jnp.sum(e, axis=0, keepdims=True)
            weighted = weighted + jnp.sum(e * dp, axis=0, keepdims=True)
            expo[h, t] = e
            dprobs[h, t] = dp
        inverse = 1.0 / total
        stats[h, 0] = inverse
        stats[h, 1] = inverse * shrink
        stats[h, 2] = weighted * inverse

    def grads(t):
        turn = turned[t]
        grad_k = grad_v = None
        for h in range(4):
            q, do = qs[h], dos[h]
            p = expo[h, t] * stats[h, 1 if t == 3 else 0]
            ds = (p * (dprobs[h, t] - stats[h, 2])).astype(BF16)
            v = jnp.dot(p.astype(BF16), do, preferred_element_type=F32)
            k = jnp.dot(ds, q, preferred_element_type=F32)
            g = jnp.dot(turn, ds, preferred_element_type=F32)
            grad_v = v if h == 0 else grad_v + v
            grad_k = k if h == 0 else grad_k + k
            if t == 0:
                gq_sum[h] = g
            elif t < 3:
                gq_sum[h] += g
            else:
                gqs[h] = ((gq_sum[h] + g) * scaling).T.astype(BF16)
        terms[t, 0] = (grad_k * scaling).astype(BF16).reshape(2, 4, rows, feature)
        terms[t, 1] = grad_v.astype(BF16).reshape(2, 4, rows, feature)

    asks = [ask_copy(step) for step in range(1, 4)]
    for copy in asks:
        copy.start()
    for half in range(2):
        start_relay(0, 1, half)
        start_relay(1, 1, half)
    q_copies = {}
    for step in (1, 3, 2):
        q_copies[step] = (
            to_chip(step, 0, lambda peer: queries.at[peer], qs.at[chip]),
            to_chip(step, 1, lambda peer: dout.at[peer], dos.at[chip]),
        )
        for copy in q_copies[step]:
            copy.start()
    asked[y] = ask[y]
    qs[chip] = queries[chip]
    dos[chip] = dout[chip]
    for copy in asks:
        copy.wait_recv()
    serve(z)

    def attend_arrived(step):
        for copy in q_copies[step]:
            copy.wait_recv()
        attend_own(lax.rem(chip + 4 - step, 4))

    for hop in range(1, reach + 1):
        near = z - hop
        far = lax.rem(z + hop, nz)
        for half in range(2):

            @pl.when(near >= 0)
            def _():
                relay(near, half, 0, 2).wait_recv()

            if hop < reach:
                start_relay(0, hop + 1, half)
            if hop <= wrap:

                @pl.when(far <= wrap - 1)
                def _():
                    relay(far, half, 1, 2).wait_recv()

                if hop < wrap:
                    start_relay(1, hop + 1, half)

        @pl.when(near >= 0)
        def _():
            serve(near)

        if hop <= wrap:

            @pl.when(jnp.logical_and(far <= wrap - 1, far < z))
            def _():
                serve(far)

        if hop == 1:
            attend_own(chip)
            turned[3] = key_rows(3).T
        elif hop == reach - 1:
            attend_arrived(1)
    attend_arrived(3)

    def got_slots(source, carry):
        for step in range(1, 4):
            slot_copy(step, source).wait_recv()
        return carry

    lax.fori_loop(0, z + 1, got_slots, 0)

    for x in range(4):
        for t in range(3):
            comp[x, t] = pool[cidx[x * 3 + t]]
    kv_copies = {
        step: to_chip(step, 2, lambda peer: comp.at[peer], near_kv.at[:, :, core, chip])
        for step in (1, 3, 2)
    }
    for copy in kv_copies.values():
        copy.start()
    for t in range(3):
        for half in range(2):
            near_kv[t, half, core, chip] = comp[chip, t, half]
    swaps = [to_core(0, comp.at[chip], near_kv.at[:, :, core, chip])]
    swaps[0].start()
    attend_arrived(2)
    for step, copy in kv_copies.items():
        copy.wait_recv()
        piece = near_kv.at[:, :, core, lax.rem(chip + 4 - step, 4)]
        swaps.append(to_core(step, piece, piece))
        swaps[-1].start()
    for x in range(4):
        incoming[x, 3] = jnp.zeros_like(incoming[x, 3])
    for owner in range(nz):
        sums[owner] = jnp.zeros_like(sums[owner])
    for copy in swaps:
        copy.wait_recv()

    for t in range(3):
        turned[t] = key_rows(t).T

    def far_head(h, carry):
        attend_far(h)
        return carry

    lax.fori_loop(0, 4, far_head, 0)

    merges = [to_core(4 + t, terms.at[t, :, 1 - core], pair.at[t]) for t in range(4)]

    def spread_copies(t):
        there = own_in.at[chip] if t == 3 else incoming.at[chip, t]
        return [to_chip(step, 3 + t, lambda peer: outgoing.at[peer, t], there) for step in (1, 3, 2)]

    spreads = [spread_copies(t) for t in range(4)]

    def combine(t):
        merges[t].wait_recv()
        for half in range(2):
            for x in range(4):
                total = terms[t, half, core, x].astype(F32) + pair[t, half, x].astype(F32)
                outgoing[x, t, half] = total.astype(BF16)
        for copy in spreads[t]:
            copy.start()
        if t == 3:
            own_in[chip] = outgoing[chip, t]
        else:
            incoming[chip, t] = outgoing[chip, t]

    for t in range(3):
        grads(t)
        merges[t].start()
        if t > 0:
            combine(t - 1)
    combine(2)
    grads(3)
    merges[3].start()
    gq_copies = [
        to_chip(step, 7, lambda peer: gqs.at[peer], gq_out.at[chip]) for step in (1, 3, 2)
    ]
    for t in range(3):
        for copy in spreads[t]:
            copy.wait_recv()

    def give_copy(step, owner):
        return pltpu.make_async_remote_copy(
            src_ref=y_out.at[step, owner],
            dst_ref=y_in.at[step, owner],
            send_sem=back_y_send.at[step, owner],
            recv_sem=back_y_recv.at[step, owner],
            device_id={"ctx": z * 4 + lax.rem(y + step, 4)},
            device_id_type=MESH,
        )

    def reduce_copy(owner, half, back):
        peer = lax.rem(z + 1, nz) if back else lax.rem(z + nz - 1, nz)
        return pltpu.make_async_remote_copy(
            src_ref=z_out.at[owner, half],
            dst_ref=z_in.at[back, owner, half],
            send_sem=back_z_send.at[owner, half],
            recv_sem=back_z_recv.at[back, owner, half],
            device_id={"ctx": peer * 4 + y},
            device_id_type=MESH,
        )

    def collect(spot):
        total = None
        for x in range(4):
            which = 3
            for t in range(3):
                which = jnp.where(code[3 * x + t] == spot, t, which)
            term = incoming[x, which].astype(F32)
            total = term if total is None else total + term
        return total

    def give(owner):
        for step in range(4):
            y_out[step, owner] = collect(4 * owner + lax.rem(y + step, 4)).astype(BF16)
        for step in range(1, 4):
            give_copy(step, owner).start()

    def gather(owner):
        for step in range(1, 4):
            give_copy(step, owner).wait_recv()
        masks = []
        for step in range(4):
            wish = jnp.broadcast_to(asked[lax.rem(y + 4 - step, 4), pl.ds(owner, 1)], (16, 128))
            masks.append([jnp.where(wish == b, 1.0, 0.0) for b in range(4)])
        for half in range(2):
            for g in range(rows // 16):
                span = pl.ds(16 * g, 16)
                parts = [y_out[0, owner, half, span].astype(F32)]
                for step in range(1, 4):
                    parts.append(y_in[step, owner, half, span].astype(F32))
                for b in range(4):
                    total = parts[0] * masks[0][b]
                    for step in range(1, 4):
                        total = total + parts[step] * masks[step][b]
                    sums[owner, half, b, span] = total

    def pass_on(owner, half, back, last):
        if last:
            z_out[owner, half] = sums[owner, half].astype(BF16)
        elif back:
            reduce_copy(owner, half, back).wait_recv()
            z_out[owner, half] = (
                sums[owner, half] + z_in[back, owner, half].astype(F32)
            ).astype(BF16)
        else:

            @pl.when(z <= nz - 2)
            def _():
                reduce_copy(owner, half, back).wait_recv()
                z_out[owner, half] = (
                    sums[owner, half] + z_in[back, owner, half].astype(F32)
                ).astype(BF16)

            @pl.when(z == nz - 1)
            def _():
                z_out[owner, half] = sums[owner, half].astype(BF16)

        reduce_copy(owner, half, back).start()

    steps = []
    for i in range(reach):
        near = z - (reach - i)
        steps.append((near, near >= 0, near >= 0, 0, i == 0))
        if i < wrap:
            far = lax.rem(z + wrap - i, nz)
            needed = far <= wrap - 1
            steps.append((far, needed, jnp.logical_and(needed, far < z), 1, i == 0))
    for owner, _, mine, _, _ in steps:

        @pl.when(mine)
        def _():
            give(owner)

    give(z)
    combine(3)
    for copy in gq_copies:
        copy.start()
    gq_out[chip] = gqs[chip]
    for owner, needed, mine, back, last in steps:

        @pl.when(mine)
        def _():
            gather(owner)

        @pl.when(needed)
        def _():
            for half in range(2):
                pass_on(owner, half, back, last)

    gather(z)
    for copy in spreads[3]:
        copy.wait_recv()
    for b in range(4):
        near_sum = collect(n + b) + own_in[b].astype(F32)
        for half in range(2):
            sums[z, half, b] += near_sum[half]
    shares, tails = {}, []
    outs = (gk_out, gv_out)
    for half in range(2):

        @pl.when(z <= nz - 2)
        def _():
            reduce_copy(z, half, 0).wait_recv()
            sums[z, half] += z_in[0, z, half].astype(F32)

        @pl.when(z <= wrap - 1)
        def _():
            reduce_copy(z, half, 1).wait_recv()
            sums[z, half] += z_in[1, z, half].astype(F32)

        final[half] = sums[z, half].astype(BF16)
        for step in (1, 3, 2):
            copy = to_chip(step, 8 + half, lambda peer: final.at[half], outs[half].at[:, core, chip])
            copy.start()
            shares[half, step] = copy
        tails.append(to_core(8 + 4 * half, final.at[half], outs[half].at[:, core, chip]))
        tails[-1].start()
        for b in range(4):
            outs[half][b, core, chip] = final[half, b]
    for half in range(2):
        for step in (1, 3, 2):
            shares[half, step].wait_recv()
            piece = outs[half].at[:, core, lax.rem(chip + 4 - step, 4)]
            tails.append(to_core(8 + 4 * half + step, piece, piece))
            tails[-1].start()

    for copy in asks + list(kv_copies.values()) + swaps + merges + list(shares.values()):
        copy.wait_send()
    for pairs in q_copies.values():
        for copy in pairs:
            copy.wait_send()
    for t in range(4):
        for copy in spreads[t]:
            copy.wait_send()
    for back, last in ((0, reach), (1, wrap)):
        for hop in range(1, last + 1):
            source, needed = (backward_source if back else forward_source)(hop)
            for half in range(2):

                @pl.when(needed)
                def _():
                    relay(source, half, back, hop).wait_send()

    for owner, needed, _, back, _ in steps:

        @pl.when(needed)
        def _():
            for half in range(2):
                reduce_copy(owner, half, back).wait_send()

    def sent_slots(owner, carry):
        for step in range(1, 4):
            slot_copy(step, owner).wait_send()
            give_copy(step, owner).wait_send()
        return carry

    lax.fori_loop(0, z + 1, sent_slots, 0)
    for copy in gq_copies + tails:
        copy.wait()


def body(queries, keys, values, dout, selected):
    tok, _, feature = queries.shape
    blocks = selected.shape[0]
    length = tok // blocks
    rows = length // 8
    n = lax.axis_size("ctx")
    nz = n // 4
    scaling = 1.0 / math.sqrt(feature)
    dma = pltpu.SemaphoreType.DMA
    heads = (4, length, feature)
    slab = (rows, feature)
    part_shape = jax.ShapeDtypeStruct((blocks, 2, 4, *slab), BF16)
    gq, gk, gv = pl.pallas_call(
        functools.partial(kernel, nz, scaling),
        out_shape=(jax.ShapeDtypeStruct(heads, BF16), part_shape, part_shape),
        in_specs=[SM, VM, VM, VM, VM],
        out_specs=(VM, VM, VM),
        scratch_shapes=[
            pltpu.VMEM((4, nz, 128), F32),
            pltpu.VMEM((4, nz, 128), F32),
            pltpu.VMEM((2 * n, 2, *slab), BF16),
            pltpu.VMEM((3, nz, 2, *slab), BF16),
            pltpu.VMEM((4, 3, 2, *slab), BF16),
            pltpu.VMEM((3, 2, 2, 4, *slab), BF16),
            pltpu.VMEM(heads, BF16),
            pltpu.VMEM(heads, BF16),
            pltpu.VMEM((4, 4, length, length), F32),
            pltpu.VMEM((4, 4, length, length), F32),
            pltpu.VMEM((4, 3, 1, length), F32),
            pltpu.VMEM((4, 3, 1, length), F32),
            pltpu.VMEM((4, feature, length), BF16),
            pltpu.VMEM((4, feature, length), F32),
            pltpu.VMEM(heads, BF16),
            pltpu.VMEM((4, 2, 2, 4, *slab), BF16),
            pltpu.VMEM((4, 2, 4, *slab), BF16),
            pltpu.VMEM((4, 4, 2, *slab), BF16),
            pltpu.VMEM((4, 4, 2, *slab), BF16),
            pltpu.VMEM((4, 2, *slab), BF16),
            pltpu.VMEM((4, nz, 2, *slab), BF16),
            pltpu.VMEM((4, nz, 2, *slab), BF16),
            pltpu.VMEM((nz, 2, 4, *slab), F32),
            pltpu.VMEM((nz, 2, 4, *slab), BF16),
            pltpu.VMEM((2, nz, 2, 4, *slab), BF16),
            pltpu.VMEM((2, 4, *slab), BF16),
            dma((4,)),
            dma((4,)),
            dma((2, nz // 2, 2)),
            dma((nz, 2)),
            dma((3, nz)),
            dma((3, nz)),
            dma((10, 4)),
            dma((10, 4)),
            dma((16,)),
            dma((16,)),
            dma((4, nz)),
            dma((4, nz)),
            dma((nz, 2)),
            dma((2, nz, 2)),
        ],
        compiler_params=pltpu.CompilerParams(
            collective_id=0, has_side_effects=True, vmem_limit_bytes=62 * 2**20
        ),
        name="whole",
    )(
        selected,
        keys.reshape(blocks, 8, *slab),
        values.reshape(blocks, 8, *slab),
        queries.reshape(heads),
        dout.reshape(heads),
    )
    return (
        gq.reshape(queries.shape),
        gk.reshape(keys.shape),
        gv.reshape(values.shape),
    )


def solution(mesh):
    return jax.shard_map(
        body,
        mesh=mesh,
        in_specs=(
            P("ctx", "head", None),
            P("ctx", None),
            P("ctx", None),
            P("ctx", "head", None),
            P("ctx", None),
        ),
        out_specs=(P("ctx", "head", None), P("ctx", None), P("ctx", None)),
        check_vma=False,
    )
```

time: 113 us -> 88.3 us (0.78)
  Pallas kernels: 104 us -> 83.5 us
  local copies, waits for them, and re-layouts: 7.15 us -> 3.95 us
    pallas_call x3 -> x1, Pallas kernels: 104 us -> 83.5 us  [body(): pl.pallas_call(functools.partial(kernel, nz, scaling), out_shape=(jax.Sha...]
    reshape x2 -> x0, local copies, waits for them, and re-layouts: 1.27 us -> none  [the longest x1 0.65 us: body(): tix = jnp.concatenate([far_t, near_t], axis=1).reshape(-1)]
    unnamed x9 -> x7, local copies, waits for them, and re-layouts: 4.63 us -> 3.95 us
where the time goes in v3:
time: 88.3 us; the launch traced here: 88.1 us
  Pallas kernels  83.5 us (95%)
  local copies, waits for them, and re-layouts  3.95 us (4%)
    pallas_call x1, Pallas kernels, body(): pl.pallas_call(functools.partial(kernel, nz, scaling), out_shape=(jax.Sha...  83.5 us
    unnamed x7, local copies, waits for them, and re-layouts  3.95 us

profile of v3, /device:TPU:1, one launch (start us, length us, event | category | flops | bytes accessed | tf_op | source)
XLA Modules:
  0.0 88.1 jit_solution(9635305457284710860)
XLA Ops:
  0.6 83.5 %whole.1 = (bf16[4,512,128]{2,1,0:T(8,128)(2,1)}, bf16[4,2,4,64,128]{4,3,2,1,0:T(8,128)(2,1)}, bf16[4,2,4,64,128]{4,3,2,1,0:T(8,128)(2,1)}) custom-call(s32[4,3]{1,0:T(4,128)} %selected.1, bf16[4,8,64,128]{3,2,1,0:T(8,128)(2,1)} %bitcast.7, bf16[4,8,64,128]{3,2,1,0:T(8,128)(2,1)} %bitcast.8, bf16[4,512,128]{2,1,0:T(8,128)(2,1)} %bitcast.9, ...), custom_call_target="tpu_custom_call" | custom-call | tf_op jit(solution)/shard_map/whole/pallas_call | solution.py:617
  84.1 0.0 copy-start.1
  84.1 1.9 %copy.11 = bf16[2048,1,128]{2,0,1:T(8,128)(2,1)} copy(bf16[2048,1,128]{2,0,1:T(8,128)(2,1)} %bitcast.13) | data formatting | bytes 1048576
  86.1 0.0 copy-done.1
  86.1 0.0 copy-start
  86.1 0.8 copy.12
  86.9 0.4 copy-done
  87.3 0.8 copy.13
Async XLA Ops:
  84.1 1.9 %copy-start.1 = (bf16[4,2,4,64,128]{4,3,2,1,0:T(8,128)(2,1)S(1)}, bf16[4,2,4,64,128]{4,3,2,1,0:T(8,128)(2,1)}, u32[]{:S(2)}) copy-start(bf16[4,2,4,64,128]{4,3,2,1,0:T(8,128)(2,1)} %get-tuple-element.7) | copy-start | bytes 1572868
  86.1 1.2 %copy-start = (bf16[4,2,4,64,128]{4,3,2,1,0:T(8,128)(2,1)S(1)}, bf16[4,2,4,64,128]{4,3,2,1,0:T(8,128)(2,1)}, u32[]{:S(2)}) copy-start(bf16[4,2,4,64,128]{4,3,2,1,0:T(8,128)(2,1)} %get-tuple-element.8) | copy-start | bytes 1572868
